TPU v7x, 512 devices: a whole 4x4x16 slice. The times are simulated.
512 devices in a mesh: seq: 32 (over z, core), mp: 16 (over y, x).
Axes of the slice: x: 4, y: 4, z: 16, core: 2. Of those that a mesh axis runs over, the one named last changes fastest.
Arguments:
- continued_prompt_entries: bfloat16 [4096, 4096], P('seq', 'mp'), may hold values from -6 to 6
- padded_prompt_entries: bfloat16 [4096, 4096], P('seq', 'mp'), may hold values from -6 to 6
- prompt_live_extents: int32 [64], P('seq'), may hold values from 8 to 64, as said below
- preceding_entry_line: bfloat16 [4096], P('mp'), may hold values from -6 to 6
- carried_memory: float32 [64, 64, 64], P('mp'), may hold values from -24 to 24
- token_mixing_ratios: float32 [5, 4096], replicated, may hold values from 0.05 to 0.95
- acceptance_transform: bfloat16 [4096, 4096], P('seq', 'mp'), may hold values from -0.09375 to 0.09375
- lookup_transform: bfloat16 [4096, 4096], P('seq', 'mp'), may hold values from -0.09375 to 0.09375
- payload_transform: bfloat16 [4096, 4096], P('seq', 'mp'), may hold values from -0.09375 to 0.09375
- gating_transform: bfloat16 [4096, 4096], P('seq', 'mp'), may hold values from -0.09375 to 0.09375
- fading_baseline: float32 [4096], P('mp'), may hold values from -10 to -3.5
- fading_left_factor: bfloat16 [4096, 128], replicated, may hold values from -0.09375 to 0.09375
- fading_right_factor: bfloat16 [128, 4096], P(None, 'mp'), may hold values from -0.5 to 0.5
- present_reward: float32 [64, 64], P('mp'), may hold values from -3 to 3
- group_layer_scaling: float32 [4096], P('mp'), may hold values from 0.5 to 1.5
- group_layer_shift_term: float32 [4096], P('mp'), may hold values from -1.8 to 1.8
- final_transform: bfloat16 [4096, 4096], P('mp', 'seq'), may hold values from -0.09375 to 0.09375
Outputs:
- mixed: bfloat16 [32, 256, 4096], P('seq', 'mp')
- span_states: float32 [32, 64, 64, 64], P('seq', 'mp')
- request_states: float32 [64, 64, 64, 64], P('seq', 'mp')
Inputs may be any that keep to these rules, and one draw needn't show every extreme that they name: `prompt_live_extents`: some request has all 64 rows live.
All inputs are finite; a program needn't handle non-finite values.
Results may differ from a plain program's by a relative error of at most 0.0076.
Values may be sent and summed in bfloat16 or wider, within the bound.
A program may use at most 64 MiB of HBM per device.

v0:
```python
import jax
import jax.numpy as jnp
from jax import lax
from jax.sharding import PartitionSpec as P

BLK = 64
norm_eps = 0.00064
highest = lax.Precision.HIGHEST


def passed_along(x, axis, by):
    length = lax.axis_size(axis)
    pairs = [(i, i + by) for i in range(length) if 0 <= i + by < length]
    return lax.ppermute(x, axis, pairs)


def entering(value, axis, join, neutral):
    count, mine = (lax.axis_size(axis), lax.axis_index(axis))
    pieces = jax.tree.map(lambda part: lax.all_gather(part, axis), value)
    total = jax.tree.map(
        lambda part, zero: jnp.full_like(part, 0) + jnp.asarray(zero, part.dtype), value, neutral
    )

    def hop(position, total):
        longer = join(total, jax.tree.map(lambda part: part[position], pieces))
        return jax.tree.map(lambda new, old: jnp.where(position < mine, new, old), longer, total)

    return lax.fori_loop(0, count - 1, hop, total)


def mix_rows(current, previous, weight):
    here = current.astype(jnp.float32)
    return (here + weight[None, :] * (previous.astype(jnp.float32) - here)).astype(jnp.bfloat16)


def block_sweep(
    evolving_memory,
    acceptance_entries,
    lookup_entries,
    payload_entries,
    log_fading_amount,
    diagonal_reward,
):
    inclusive = jnp.cumsum(log_fading_amount, axis=0)
    exclusive = inclusive - log_fading_amount
    recept_scaled = acceptance_entries * jnp.exp(exclusive)
    keys_scaled = lookup_entries * jnp.exp(-inclusive)
    scores = jnp.einsum("ihc,jhc->hij", recept_scaled, keys_scaled, precision=highest)
    count = acceptance_entries.shape[0]
    row_index = lax.broadcasted_iota(jnp.int32, (count, count), 0)
    col_index = lax.broadcasted_iota(jnp.int32, (count, count), 1)
    scores = jnp.where((row_index > col_index)[None], scores, 0.0)
    diagonal_contribution = jnp.sum(
        acceptance_entries * diagonal_reward[None] * lookup_entries, axis=-1, keepdims=True
    )
    answer_lines = (
        jnp.einsum("hij,jhd->ihd", scores, payload_entries, precision=highest)
        + diagonal_contribution * payload_entries
    )
    answer_lines = answer_lines + jnp.einsum(
        "ihc,hcd->ihd", recept_scaled, evolving_memory, precision=highest
    )
    total = inclusive[-1]
    carried = lookup_entries * jnp.exp(total[None] - inclusive)
    new_state = jnp.exp(total)[:, :, None] * evolving_memory + jnp.einsum(
        "jhc,jhd->hcd", carried, payload_entries, precision=highest
    )
    return (new_state, answer_lines)


def continued_recurrence(
    acceptance_entries, lookup_entries, payload_entries, log_fading_amount, diagonal_reward
):
    length, per_group_view, embedding_dimension = acceptance_entries.shape
    blocks = length // BLK

    def step(evolving_memory, entry_lines):
        return block_sweep(
            evolving_memory,
            entry_lines[0],
            entry_lines[1],
            entry_lines[2],
            entry_lines[3],
            diagonal_reward,
        )

    shaped = tuple(
        (
            a.reshape(blocks, BLK, per_group_view, embedding_dimension)
            for a in (acceptance_entries, lookup_entries, payload_entries, log_fading_amount)
        )
    )
    evolving_memory, results = lax.scan(
        step,
        jnp.zeros((per_group_view, embedding_dimension, embedding_dimension), jnp.float32),
        shaped,
    )
    return (evolving_memory, results.reshape(length, per_group_view, embedding_dimension))


def combine(earlier, later):
    return (earlier[0] + later[0], jnp.exp(later[0])[:, :, None] * earlier[1] + later[1])


def shifted_rows(current, edge_row, long_rows, requests, slot_rows):
    feature_part = current.shape[1]
    long_prev = jnp.concatenate([edge_row, current[: long_rows - 1]], axis=0)
    short_view = current[long_rows:].reshape(requests, slot_rows, feature_part)
    short_prev = jnp.concatenate(
        [jnp.zeros((requests, 1, feature_part), current.dtype), short_view[:, :-1]], axis=1
    )
    short_prev = short_prev.reshape(requests * slot_rows, feature_part)
    return jnp.concatenate([long_prev, short_prev], axis=0)


def on_device(
    continued_prompt_entries,
    padded_prompt_entries,
    prompt_live_extents,
    preceding_entry_line,
    carried_memory,
    token_mixing_ratios,
    acceptance_transform,
    lookup_transform,
    payload_transform,
    gating_transform,
    fading_baseline,
    fading_left_factor,
    fading_right_factor,
    present_reward,
    group_layer_scaling,
    group_layer_shift_term,
    final_transform,
):
    long_rows = continued_prompt_entries.shape[0]
    requests = prompt_live_extents.shape[0]
    slot_rows = padded_prompt_entries.shape[0] // requests
    per_group_view, embedding_dimension = present_reward.shape
    arrived = passed_along(continued_prompt_entries[-1:], "seq", 1)
    first = lax.axis_index("seq") == 0
    edge_row = jnp.where(first, preceding_entry_line[None, :], arrived)
    current = jnp.concatenate([continued_prompt_entries, padded_prompt_entries], axis=0)
    current, edge_full = (
        lax.all_gather(current, "mp", axis=1, tiled=True),
        lax.all_gather(edge_row, "mp", axis=1, tiled=True),
    )
    previous = shifted_rows(current, edge_full, long_rows, requests, slot_rows)
    mixes = [mix_rows(current, previous, token_mixing_ratios[index]) for index in range(5)]
    total_rows = current.shape[0]
    columns = acceptance_transform.shape[1]
    pieces = (
        lax.all_gather(acceptance_transform, "seq", axis=0, tiled=True),
        lax.all_gather(lookup_transform, "seq", axis=0, tiled=True),
        lax.all_gather(payload_transform, "seq", axis=0, tiled=True),
        lax.all_gather(gating_transform, "seq", axis=0, tiled=True),
    )
    acceptance_entries, lookup_entries, payload_entries, gate = tuple(
        (
            jnp.dot(source, piece, preferred_element_type=jnp.float32)
            for source, piece in zip(mixes[:4], pieces)
        )
    )
    squeezed = jnp.tanh(
        jnp.dot(mixes[4], fading_left_factor, preferred_element_type=jnp.float32)
    ).astype(jnp.bfloat16)
    log_fading_amount = -jnp.exp(
        fading_baseline[None, :]
        + jnp.dot(squeezed, fading_right_factor, preferred_element_type=jnp.float32)
    )
    recept3, keys3, values3, decay3 = [
        a.reshape(total_rows, per_group_view, embedding_dimension)
        for a in (acceptance_entries, lookup_entries, payload_entries, log_fading_amount)
    ]
    local_state, long_out = continued_recurrence(
        recept3[:long_rows],
        keys3[:long_rows],
        values3[:long_rows],
        decay3[:long_rows],
        present_reward,
    )
    long_decay = decay3[:long_rows]
    group_total = jnp.sum(long_decay, axis=0)
    blank = (
        jnp.zeros((per_group_view, embedding_dimension), jnp.float32),
        jnp.zeros((per_group_view, embedding_dimension, embedding_dimension), jnp.float32),
    )
    prefix_total, prefix_state = entering((group_total, local_state), "seq", combine, blank)
    incoming = jnp.exp(prefix_total)[:, :, None] * carried_memory + prefix_state
    before_row = jnp.cumsum(long_decay, axis=0) - long_decay
    long_out = long_out + jnp.einsum(
        "ihc,hcd->ihd", recept3[:long_rows] * jnp.exp(before_row), incoming, precision=highest
    )
    span_end = jnp.exp(group_total)[:, :, None] * incoming + local_state
    live_rows = (
        lax.broadcasted_iota(jnp.int32, (requests, slot_rows), 1) < prompt_live_extents[:, None]
    )
    live_flat = live_rows.reshape(requests * slot_rows).astype(jnp.float32)[:, None, None]
    short_shape = (requests, slot_rows, per_group_view, embedding_dimension)
    short_recept = recept3[long_rows:].reshape(short_shape)
    short_keys = (keys3[long_rows:] * live_flat).reshape(short_shape)
    short_values = values3[long_rows:].reshape(short_shape)
    short_decay = (decay3[long_rows:] * live_flat).reshape(short_shape)
    zeroed_memory = jnp.zeros(
        (per_group_view, embedding_dimension, embedding_dimension), jnp.float32
    )

    def request_pass(acceptance_lines, lookup_table, payload_table, fading_table):
        return block_sweep(
            zeroed_memory,
            acceptance_lines,
            lookup_table,
            payload_table,
            fading_table,
            present_reward,
        )

    request_states, short_out = jax.vmap(request_pass)(
        short_recept, short_keys, short_values, short_decay
    )
    wkv = jnp.concatenate(
        [long_out, short_out.reshape(requests * slot_rows, per_group_view, embedding_dimension)],
        axis=0,
    )
    mean = jnp.mean(wkv, axis=-1, keepdims=True)
    centred = wkv - mean
    variance = jnp.mean(centred * centred, axis=-1, keepdims=True)
    normed = (centred * lax.rsqrt(variance + norm_eps)).reshape(
        total_rows, columns
    ) * group_layer_scaling[None, :] + group_layer_shift_term[None, :]
    row_live = jnp.concatenate(
        [jnp.ones((long_rows,), dtype=bool), live_rows.reshape(requests * slot_rows)], axis=0
    )
    hidden = jnp.where(row_live[:, None], normed * jax.nn.silu(gate), 0.0).astype(jnp.bfloat16)
    full_out = lax.all_gather(final_transform, "seq", axis=1, tiled=True)
    mixed_rows = lax.psum_scatter(
        jnp.dot(hidden, full_out, preferred_element_type=jnp.float32),
        "mp",
        scatter_dimension=0,
        tiled=True,
    )
    return (mixed_rows.astype(jnp.bfloat16)[None], span_end[None], request_states)


def solution(mesh):
    placed = (
        P("seq", "mp"),
        P("seq", "mp"),
        P("seq"),
        P("mp"),
        P("mp", None, None),
        P(),
        P("seq", "mp"),
        P("seq", "mp"),
        P("seq", "mp"),
        P("seq", "mp"),
        P("mp"),
        P(),
        P(None, "mp"),
        P("mp", None),
        P("mp"),
        P("mp"),
        P("mp", "seq"),
    )
    return jax.shard_map(
        on_device,
        mesh=mesh,
        in_specs=placed,
        out_specs=(P("seq", "mp", None), P("seq", "mp", None, None), P("seq", "mp", None, None)),
        check_vma=False,
    )
```

profile of v0, /device:TPU:2, one launch (start us, length us, event | category | flops | bytes accessed | tf_op | source)
XLA Modules:
  0.0 631.1 jit_solution(9215683122175775181)
XLA Ops:
  7.2 1.6 pad_maximum_fusion.2
  11.7 1.7 collective-permute-start
  13.4 1.9 fusion.85
  16.0 27.3 %all_gather.34 = bf16[1,4096]{1,0:T(2,128)(2,1)} all-gather(bf16[1,256]{1,0:T(2,128)(2,1)S(1)} %broadcast_select_fusion), channel_id=1, replica_groups=mesh['seq'=32,'mp'=16] {'mp'}, dimensions={1}, use_global_device_ids=true | all-gather | bytes 8704 | tf_op jit(solution)/shard_map/all_gather | solution.py:145
  43.3 35.5 %all-gather.9.cloned.1.call-done = bf16[256,4096]{1,0:T(8,128)(2,1)} async-done(((bf16[256,256]{1,0:T(8,128)(2,1)}), bf16[256,4096]{1,0:T(8,128)(2,1)}) %all-gather.9.cloned.1.call-update) | async-done | bytes 2097168 | tf_op jit(solution)/shard_map/all_gather | solution.py:144
  78.7 1.5 slice.100
  80.2 1.2 concatenate.24
  81.4 1.1 slice.99
  82.5 3.0 fusion.41
  85.5 1.3 slice_reduce_fusion
  86.8 1.1 reshape.138
  87.9 64.6 %all-gather.15.cloned.1.call-done = bf16[4096,256]{1,0:T(8,128)(2,1)} async-done(((bf16[128,256]{1,0:T(8,128)(2,1)}), bf16[4096,256]{1,0:T(8,128)(2,1)}) %all-gather.15.cloned.1.call-update) | async-done | bytes 2097168 | tf_op jit(solution)/shard_map/all_gather | solution.py:152
  152.5 3.7 fusion.25
  157.0 66.3 %all-gather.11.cloned.1.call-done = bf16[4096,256]{1,0:T(8,128)(2,1)} async-done(((bf16[128,256]{1,0:T(8,128)(2,1)}), bf16[4096,256]{1,0:T(8,128)(2,1)}) %all-gather.11.cloned.1.call-update) | async-done | bytes 2097168 | tf_op jit(solution)/shard_map/all_gather | solution.py:153
  223.3 4.0 fusion.29
  228.2 65.8 %all-gather.13.cloned.1.call-done = bf16[4096,256]{1,0:T(8,128)(2,1)} async-done(((bf16[128,256]{1,0:T(8,128)(2,1)}), bf16[4096,256]{1,0:T(8,128)(2,1)}) %all-gather.13.cloned.1.call-update) | async-done | bytes 2097168 | tf_op jit(solution)/shard_map/all_gather | solution.py:154
  294.0 3.6 fusion.27
  298.5 13.3 %while.29 = (s32[]{:T(128)}, f32[4,64,64]{2,1,0:T(8,128)S(1)}, f32[2,64,4,64]{1,0,3,2:T(2,128)}, f32[2,64,4,64]{1,0,3,2:T(2,128)S(1)}, f32[2,64,4,64]{3,2,1,0:T(...) while((s32[]{:T(128)}, f32[4,64,64]{2,1,0:T(8,128)S(1)}, ...), condition=%wide.region_3.4_spmd.clone, body=%wide.region_0.3_spmd.clone.sunk | while | flops 51646208 | bytes 2444416 | solution.py:93
  300.4 4.3 dynamic_update_slice.6
  307.1 4.3 dynamic_update_slice.6
  314.7 32.2 %all_gather.39 = f32[32,4,64]{2,1,0:T(4,128)} all-gather(f32[1,4,64]{2,1,0:T(4,128)S(1)} %all_gather.38), channel_id=1, replica_groups=mesh['seq'=32,'mp'=16] {'seq'}, dimensions={0}, use_global_device_ids=true | all-gather | bytes 33792 | tf_op jit(solution)/shard_map/all_gather | solution.py:19
  347.6 1.2 reshape.144
  348.9 1.1 slice.94
  350.0 1.1 exponential_multiply_fusion
  351.2 1.1 reshape.143
  358.3 25.6 %all-gather.21.cloned.1.call-done = f32[128,64,64]{2,1,0:T(8,128)} async-done(((f32[4,64,64]{2,1,0:T(8,128)}), f32[128,64,64]{2,1,0:T(8,128)}) %all-gather.21.cloned.1.call-update) | async-done | bytes 2097168 | tf_op jit(solution)/shard_map/all_gather | solution.py:19
  383.9 53.9 %while.30 = (s32[]{:T(128)}, f32[4,64]{1,0:T(4,128)S(1)}, f32[4,64,64]{2,1,0:T(8,128)S(1)}, s32[]{:T(128)}, f32[32,4,64]{2,1,0:T(4,128)}, /*index=5*/f32[32,4,64,64]{3,2,1,0:T(8,128)}, s32[]{:T(128)}, s32[]{:T(128)}) while((s32[]{:T(128)}, f32[4,64]{1,0:T(4,128)S(1)}, f32[4,64,64]{2,1,0:T(8,128)S(1)}, s32[]{:T(128)}, ...), condition=%wide.region_6.7_spmd.clone, body=%wide.region_5.6_spmd.clone.sunk | while | flops 66308 | bytes 201843 | solution.py:28
  384.5 1.0 fusion.119
  386.2 1.0 fusion.119
  387.9 1.0 fusion.119
  400.2 1.0 fusion.119
  403.7 1.0 fusion.119
  405.4 1.0 fusion.119
  407.1 1.0 fusion.119
  408.9 1.0 fusion.119
  412.3 1.0 fusion.119
  422.7 1.0 fusion.119
  428.0 1.0 fusion.119
  437.8 1.8 fusion.42
  442.3 1.8 copy.102
  444.8 1.8 copy.101
  446.5 1.7 copy.99
  448.2 5.8 all-gather.17.cloned.1.call-done
  454.0 72.6 %all-gather.19.cloned.1.call-done = bf16[256,4096]{1,0:T(8,128)(2,1)} async-done(((bf16[256,128]{1,0:T(8,128)(2,1)}), bf16[256,4096]{1,0:T(8,128)(2,1)}) %all-gather.19.cloned.1.call-update) | async-done | bytes 2097168 | tf_op jit(solution)/shard_map/all_gather | solution.py:234
  526.5 7.5 %fusion.63 = f32[256,4096]{1,0:T(8,128)} fusion(bf16[256,4096]{1,0:T(8,128)(2,1)} %all-gather.19.cloned.1.call-done, f32[256,256]{1,0:T(8,128)} %copy.102, f32[256,256]{1,0:T(8,128)} %copy.101, f32[128,256]{1,0:T(8,128)} %concatenate.27, f32[128,256]{1,0:T(8,128)} %copy.99, bf16[4096,256]{1,0:T(8,128)(2,1)} %all-gather.17.cloned.1.call-done, ...), kind=kOutput, calls=%fused_computation.83 | convolution fusion | flops 1086062592 | bytes 13388032 | tf_op jit(solution)/shard_map/dot_general | solution.py:236
  535.0 1.3 convolution_add_fusion.1
  537.1 85.6 %reduce-scatter.2.cloned.1.call-done = f32[16,4096]{1,0:T(8,128)} async-done(((f32[256,4096]{1,0:T(8,128)}), f32[16,4096]{1,0:T(8,128)}) %reduce-scatter.2.cloned.1.call-update) | async-done | bytes 262160 | tf_op jit(solution)/shard_map/reduce_scatter | solution.py:235
  622.7 1.6 convert_bitcast_fusion
  (180 shorter events, 66.9 us)
Async XLA Ops:
  7.2 75.3 %copy-start = (bf16[4096,128]{1,0:T(8,128)(2,1)S(1)}, bf16[4096,128]{1,0:T(8,128)(2,1)}, u32[]{:S(2)}) copy-start(bf16[4096,128]{1,0:T(8,128)(2,1)} %param.32) | copy-start | bytes 3145732
  7.2 71.5 %all-gather.9.cloned.1.call-start = ((), (), s32[]{:S(2)}) async-start(), calls=%async_computation.1 | async-start | bytes 2228224 | tf_op jit(solution)/shard_map/all_gather | solution.py:144
  8.9 143.6 %all-gather.15.cloned.1.call-start = ((), (), s32[]{:S(2)}) async-start(), calls=%async_computation.4 | async-start | bytes 2162688 | tf_op jit(solution)/shard_map/all_gather | solution.py:152
  9.6 213.7 %all-gather.11.cloned.1.call-start = ((), (), s32[]{:S(2)}) async-start(), calls=%async_computation.2 | async-start | bytes 2162688 | tf_op jit(solution)/shard_map/all_gather | solution.py:153
  10.4 283.7 %all-gather.13.cloned.1.call-start = ((), (), s32[]{:S(2)}) async-start(), calls=%async_computation.3 | async-start | bytes 2162688 | tf_op jit(solution)/shard_map/all_gather | solution.py:154
  10.9 372.9 %all-gather.21.cloned.1.call-start = ((), (), s32[]{:S(2)}) async-start(), calls=%async_computation.8 | async-start | bytes 4325376 | tf_op jit(solution)/shard_map/all_gather | solution.py:19
  11.7 3.7 collective-permute-start
  78.7 2.7 copy-start.3
  223.3 70.7 %copy-start.8 = (bf16[2,64,4096]{2,1,0:T(8,128)(2,1)S(1)}, bf16[2,64,4096]{2,1,0:T(8,128)(2,1)}, u32[]{:S(2)}) copy-start(bf16[2,64,4096]{2,1,0:T(8,128)(2,1)} %concatenate.24) | copy-start | bytes 3145732
  223.3 70.7 %copy-start.14 = (bf16[1,4096]{1,0:T(2,128)(2,1)S(1)}, bf16[1,4096]{1,0:T(2,128)(2,1)}, u32[]{:S(2)}) copy-start(bf16[1,4096]{1,0:T(2,128)(2,1)} %all_gather.34) | copy-start | bytes 24580
  294.0 4.5 copy-start.13
  298.5 15.4 %copy-start.16 = (s32[2]{0:T(128)S(1)}, s32[2]{0:T(128)}, u32[]{:S(2)}) copy-start(s32[2]{0:T(128)} %param.23) | copy-start | bytes 28
  298.5 16.1 %copy-start.15 = (f32[256]{0:T(256)S(1)}, f32[256]{0:T(256)}, u32[]{:S(2)}) copy-start(f32[256]{0:T(256)} %get-tuple-element.272) | copy-start | bytes 3076
  298.5 48.3 %copy-start.6 = (f32[128,256]{0,1:T(8,128)S(1)}, f32[128,256]{0,1:T(8,128)}, u32[]{:S(2)}) copy-start(f32[128,256]{0,1:T(8,128)} %get-tuple-element.274) | copy-start | bytes 393220
  298.5 48.5 %copy-start.10 = (f32[128,256]{0,1:T(8,128)S(1)}, f32[128,256]{0,1:T(8,128)}, u32[]{:S(2)}) copy-start(f32[128,256]{0,1:T(8,128)} %get-tuple-element.273) | copy-start | bytes 393220
  311.8 0.7 copy-start.1
  312.5 141.5 %all-gather.17.cloned.1.call-start = ((), (), s32[]{:S(2)}) async-start(), calls=%async_computation.5 | async-start | bytes 2162688 | tf_op jit(solution)/shard_map/all_gather | solution.py:155
  313.0 213.5 %all-gather.19.cloned.1.call-start = ((), (), s32[]{:S(2)}) async-start(), calls=%async_computation.6 | async-start | bytes 2162688 | tf_op jit(solution)/shard_map/all_gather | solution.py:234
  313.8 308.9 %reduce-scatter.2.cloned.1.call-start = ((), (), s32[]{:S(2)}) async-start(), calls=%async_computation.7 | async-start | bytes 4456448 | tf_op jit(solution)/shard_map/reduce_scatter | solution.py:235
  347.3 7.4 %copy-start.12 = (f32[2,64,4,64]{1,0,3,2:T(2,128)S(1)}, f32[2,64,4,64]{1,0,3,2:T(2,128)}, u32[]{:S(2)}) copy-start(f32[2,64,4,64]{1,0,3,2:T(2,128)} %get-tuple-element.156) | copy-start | bytes 393220
  347.5 5.4 copy-start.7
  354.6 171.9 %copy-start.17 = (f32[256]{0:T(256)S(1)}, f32[256]{0:T(256)}, u32[]{:S(2)}) copy-start(f32[256]{0:T(256)} %param.36) | copy-start | bytes 3076
  358.3 168.2 %copy-start.4 = (bf16[256,4096]{1,0:T(8,128)(2,1)S(1)}, bf16[256,4096]{1,0:T(8,128)(2,1)}, u32[]{:S(2)}) copy-start(bf16[256,4096]{1,0:T(8,128)(2,1)} %all-gather.9.cloned.1.call-done) | copy-start | bytes 6291460
  439.6 1.0 copy-start.5
  534.0 0.9 copy-start.9
  534.0 2.3 copy-start.2
  534.0 2.3 copy-start.11
Sparse Core Ops, SparseCore 0:
  11.6 67.0 all-gather.8
  80.8 71.5 all-gather.14
  154.6 68.6 all-gather.10
  225.3 68.6 all-gather.12
  312.6 71.2 all-gather.20
  385.8 68.0 all-gather.16
  456.0 70.4 all-gather.18
  534.2 88.4 reduce-scatter.1
where the time goes:
time: 633 us; the launch traced here: 631 us
  waiting for transfers between devices  425 us (67%)
  other arithmetic  64.5 us (10%)
  blocking collectives  59.4 us (9%)
  local copies, waits for them, and re-layouts  35.3 us (6%)
  matrix products  29.4 us (5%)
  between operations  14.5 us (2%)
    reduce_scatter x1, waiting for transfers between devices, on_device(): lax.psum_scatter(jnp.dot(hidden, full_out, preferred_element_type=jnp.flo...  85.6 us
    all_gather x1, waiting for transfers between devices, on_device(): full_out = lax.all_gather(final_transform, 'seq', axis=1, tiled=True)  72.6 us
    all_gather x1, waiting for transfers between devices, on_device(): lax.all_gather(lookup_transform, 'seq', axis=0, tiled=True)  66.3 us
    all_gather x1, waiting for transfers between devices, on_device(): lax.all_gather(payload_transform, 'seq', axis=0, tiled=True)  65.8 us
    all_gather x1, waiting for transfers between devices, on_device(): lax.all_gather(acceptance_transform, 'seq', axis=0, tiled=True)  64.6 us
    all_gather x1, waiting for transfers between devices, on_device(): lax.all_gather(current, 'mp', axis=1, tiled=True)  35.5 us
    all_gather x1, blocking collectives, entering(): pieces = jax.tree.map(lambda part: lax.all_gather(part, axis), value)  32.2 us
    select_n x31, other arithmetic, hop(): jnp.where(position < mine, new, old)  32 us
  transfers between devices with their start and end apart: 9, of which 8 were waited for; matrix products, arithmetic and copies ran while one was open for 16% of the time, Pallas kernels for 0%

commit v1 on v0

--- a/solution.py
+++ b/solution.py
@@ -6,6 +6,28 @@
 BLK = 64
 norm_eps = 0.00064
 highest = lax.Precision.HIGHEST
+
+
+def laid_out(pieces, dim):
+    pieces = jnp.moveaxis(pieces, 0, dim)
+    dims = pieces.shape
+    return pieces.reshape(*dims[:dim], dims[dim] * dims[dim + 1], *dims[dim + 2 :])
+
+
+def ring_gather(x, axis, dim):
+    size = lax.axis_size(axis)
+    pairs = [(i, (i + 1) % size) for i in range(size)]
+    back = [(b, a) for a, b in pairs]
+    lower, upper = ([], [])
+    for step in range(size - 1):
+        if step % 2 == 0:
+            lower.append(lax.ppermute(lower[-1] if lower else x, axis, pairs))
+        else:
+            upper.append(lax.ppermute(upper[-1] if upper else x, axis, back))
+    tiles = jnp.stack([*lower[::-1], x, *upper])
+    shift = lax.axis_index(axis) - len(lower)
+    tiles = tiles[(jnp.arange(size) - shift) % size]
+    return laid_out(tiles, dim)
 
 
 def passed_along(x, axis, by):
@@ -141,7 +163,7 @@
     edge_row = jnp.where(first, preceding_entry_line[None, :], arrived)
     current = jnp.concatenate([continued_prompt_entries, padded_prompt_entries], axis=0)
     current, edge_full = (
-        lax.all_gather(current, "mp", axis=1, tiled=True),
+        ring_gather(current, "mp", 1),
         lax.all_gather(edge_row, "mp", axis=1, tiled=True),
     )
     previous = shifted_rows(current, edge_full, long_rows, requests, slot_rows)

time: 633 us -> 562 us (0.89)
  waiting for transfers between devices: 425 us -> 294 us
  starting transfers between devices: 2.04 us -> 64.4 us
  other arithmetic: 64.5 us -> 56.5 us
  local copies, waits for them, and re-layouts: 35.3 us -> 42.9 us
    all_gather x1, waiting for transfers between devices: 66.3 us -> 0.01 us  [on_device(): lax.all_gather(lookup_transform, 'seq', axis=0, tiled=True)]
    all_gather x1, waiting for transfers between devices: 64.6 us -> 0.02 us  [on_device(): lax.all_gather(acceptance_transform, 'seq', axis=0, tiled=True)]
    ppermute x0 -> x15, starting transfers between devices: none -> 62.9 us  [the longest x7 46.1 us: ring_gather(): upper.append(lax.ppermute(upper[-1] if upper else x, axis, back))]
    all_gather x1 -> x0, waiting for transfers between devices: 35.5 us -> none  [on_device(): lax.all_gather(current, 'mp', axis=1, tiled=True)]
    all_gather x1, waiting for transfers between devices: 5.77 us -> 34.3 us  [on_device(): lax.all_gather(gating_transform, 'seq', axis=0, tiled=True)]
    exp x31, other arithmetic: 21 us -> 0.5 us  [combine(): jnp.exp(later[0])[:, :, None] * earlier[1] + later[1]]
    convert_element_type x0 -> x3, other arithmetic: none -> 17 us  [the longest x2 14.5 us: mix_rows(): (here + weight[None, :] * (previous.astype(jnp.float32) - here)).astype(j...]
    ppermute x0 -> x15, waiting for transfers between devices: none -> 12.9 us  [the longest x8 12.4 us: ring_gather(): lower.append(lax.ppermute(lower[-1] if lower else x, axis, pairs))]
  transfers between devices with their start and end apart: 9 -> 23, of which waited for: 8 -> 11; matrix products, arithmetic and copies ran while one was open for 16% -> 18% of each run, Pallas kernels for 0% -> 0%
where the time goes in v1:
time: 562 us; the launch traced here: 560 us
  waiting for transfers between devices  294 us (52%)
  starting transfers between devices  64.4 us (11%)
  blocking collectives  61.4 us (11%)
  other arithmetic  56.5 us (10%)
  local copies, waits for them, and re-layouts  42.9 us (8%)
  matrix products  25.4 us (5%)
  between operations  14.8 us (3%)
    reduce_scatter x1, waiting for transfers between devices, on_device(): lax.psum_scatter(jnp.dot(hidden, full_out, preferred_element_type=jnp.flo...  85.1 us
    all_gather x1, waiting for transfers between devices, on_device(): full_out = lax.all_gather(final_transform, 'seq', axis=1, tiled=True)  72.4 us
    all_gather x1, waiting for transfers between devices, on_device(): lax.all_gather(payload_transform, 'seq', axis=0, tiled=True)  53.1 us
    ppermute x7, starting transfers between devices, ring_gather(): upper.append(lax.ppermute(upper[-1] if upper else x, axis, back))  46.1 us
    all_gather x1, waiting for transfers between devices, on_device(): lax.all_gather(gating_transform, 'seq', axis=0, tiled=True)  34.3 us
    all_gather x1, waiting for transfers between devices, entering(): pieces = jax.tree.map(lambda part: lax.all_gather(part, axis), value)  33.3 us
    select_n x31, other arithmetic, hop(): jnp.where(position < mine, new, old)  32.2 us
    all_gather x1, blocking collectives, on_device(): lax.all_gather(edge_row, 'mp', axis=1, tiled=True)  31.6 us
  transfers between devices with their start and end apart: 23, of which 11 were waited for; matrix products, arithmetic and copies ran while one was open for 18% of the time, Pallas kernels for 0%

profile of v1, /device:TPU:2, one launch (start us, length us, event | category | flops | bytes accessed | tf_op | source)
XLA Modules:
  0.0 560.3 jit_solution(9588963675449022258)
XLA Ops:
  10.4 3.4 collective-permute-start
  13.8 7.3 %collective-permute-done = bf16[256,256]{1,0:T(8,128)(2,1)S(1)} collective-permute-done((bf16[256,256]{1,0:T(8,128)(2,1)S(1)}, bf16[256,256]{1,0:T(8,128)(2,1)S(1)}, u32[]{:S(2)}, u32[]{:S(2)}) %collective-permute-start) | collective-permute-done | bytes 131104 | tf_op jit(solution)/shard_map/ppermute | solution.py:24
  21.1 1.9 collective-permute-start.1
  23.1 7.2 %collective-permute-start.8 = (bf16[256,256]{1,0:T(8,128)(2,1)S(1)}, bf16[256,256]{1,0:T(8,128)(2,1)S(1)}, u32[]{:S(2)}, u32[]{:S(2)}) collective-permute-start(bf16[256,256]{1,0:T(8,128)(2,1)S(1)} %constant_dynamic-update-slice_fusion), channel_id=1, source_target_pairs={{1,0},{2,1},{3,2},{4,3},{5,4},{6,5},{7,6},{8,7},{9,8},{10,9},{11,1... | collective-permute-start | bytes 393224 | tf_op jit(solution)/shard_map/ppermute | solution.py:26
  31.3 1.9 collective-permute-start.2
  33.2 7.2 %collective-permute-start.9 = (bf16[256,256]{1,0:T(8,128)(2,1)S(1)}, bf16[256,256]{1,0:T(8,128)(2,1)S(1)}, u32[]{:S(2)}, u32[]{:S(2)}) collective-permute-start(bf16[256,256]{1,0:T(8,128)(2,1)S(1)} %collective-permute-done.8), channel_id=1, source_target_pairs={{1,0},{2,1},{3,2},{4,3},{5,4},{6,5},{7,6},{8,7},{9,8},{10,9},{11,1... | collective-permute-start | bytes 393224 | tf_op jit(solution)/shard_map/ppermute | solution.py:26
  40.5 1.8 collective-permute-done.2
  42.3 1.9 collective-permute-start.3
  44.2 7.6 %collective-permute-start.10 = (bf16[256,256]{1,0:T(8,128)(2,1)S(1)}, bf16[256,256]{1,0:T(8,128)(2,1)S(1)}, u32[]{:S(2)}, u32[]{:S(2)}) collective-permute-start(bf16[256,256]{1,0:T(8,128)(2,1)S(1)} %collective-permute-done.9), channel_id=1, source_target_pairs={{1,0},{2,1},{3,2},{4,3},{5,4},{6,5},{7,6},{8,7},{9,8},{10,9},{11,1... | collective-permute-start | bytes 393224 | tf_op jit(solution)/shard_map/ppermute | solution.py:26
  51.8 1.8 collective-permute-done.3
  53.6 1.9 collective-permute-start.4
  56.4 1.3 collective-permute-start.15
  57.8 7.0 %collective-permute-start.11 = (bf16[256,256]{1,0:T(8,128)(2,1)S(1)}, bf16[256,256]{1,0:T(8,128)(2,1)S(1)}, u32[]{:S(2)}, u32[]{:S(2)}) collective-permute-start(bf16[256,256]{1,0:T(8,128)(2,1)S(1)} %collective-permute-done.10), channel_id=1, source_target_pairs={{1,0},{2,1},{3,2},{4,3},{5,4},{6,5},{7,6},{8,7},{9,8},{10,9},{11,1... | collective-permute-start | bytes 393224 | tf_op jit(solution)/shard_map/ppermute | solution.py:26
  64.7 1.9 collective-permute-start.5
  66.7 2.1 fusion.62
  68.7 7.2 %collective-permute-start.12 = (bf16[256,256]{1,0:T(8,128)(2,1)S(1)}, bf16[256,256]{1,0:T(8,128)(2,1)S(1)}, u32[]{:S(2)}, u32[]{:S(2)}) collective-permute-start(bf16[256,256]{1,0:T(8,128)(2,1)S(1)} %collective-permute-done.11), channel_id=1, source_target_pairs={{1,0},{2,1},{3,2},{4,3},{5,4},{6,5},{7,6},{8,7},{9,8},{10,9},{11,1... | collective-permute-start | bytes 393224 | tf_op jit(solution)/shard_map/ppermute | solution.py:26
  76.0 1.9 collective-permute-start.6
  78.5 7.2 %collective-permute-start.13 = (bf16[256,256]{1,0:T(8,128)(2,1)S(1)}, bf16[256,256]{1,0:T(8,128)(2,1)S(1)}, u32[]{:S(2)}, u32[]{:S(2)}) collective-permute-start(bf16[256,256]{1,0:T(8,128)(2,1)S(1)} %collective-permute-done.12), channel_id=1, source_target_pairs={{1,0},{2,1},{3,2},{4,3},{5,4},{6,5},{7,6},{8,7},{9,8},{10,9},{11,1... | collective-permute-start | bytes 393224 | tf_op jit(solution)/shard_map/ppermute | solution.py:26
  86.2 1.9 collective-permute-start.7
  88.8 31.6 %all_gather.30 = bf16[1,4096]{0,1:T(8,128)(2,1)} all-gather(bf16[1,256]{0,1:T(8,128)(2,1)S(1)} %reshape_select_fusion), channel_id=1, replica_groups=mesh['seq'=32,'mp'=16] {'mp'}, dimensions={1}, use_global_device_ids=true | all-gather | bytes 8704 | tf_op jit(solution)/shard_map/all_gather | solution.py:167
  120.5 2.6 collective-permute-start.14
  133.7 2.3 gather_fusion
  136.0 2.5 bitcast_convert_fusion
  138.5 1.1 slice.106
  141.7 2.3 copy.122
  144.0 5.4 copy.119
  149.4 4.4 fusion.18
  153.8 2.6 fusion.26
  157.3 10.1 %fusion.22 = (bf16[256,4096]{0,1:T(8,128)(2,1)}, bf16[256,4096]{0,1:T(8,128)(2,1)}, bf16[256,4096]{0,1:T(8,128)(2,1)}, bf16[256,4096]{0,1:T(8,128)(2,1)}) fusion(f32[256,16,256]{0,2,1:T(8,128)} %copy.119, f32[4096]{0:T(1024)S(1)} %bitcast.214, bf16[128,4096]{0,1:T(8,128)(2,1)S(1)} %copy.124, bf16[127,4096]{0,1:T(8,128)(2,1)} %bitcast.204, ...), kind=kLoop, calls=%fused_computation.47 | loop fusion | flops 19922944 | bytes 14745600 | tf_op jit(solution)/shard_map/convert_element_type | solution.py:55
  167.4 3.1 fusion.67
  171.3 3.2 fusion.65
  175.1 53.1 %all-gather.10.cloned.1.call-done = bf16[4096,256]{1,0:T(8,128)(2,1)} async-done(((bf16[128,256]{1,0:T(8,128)(2,1)}), bf16[4096,256]{1,0:T(8,128)(2,1)}) %all-gather.10.cloned.1.call-update) | async-done | bytes 2097168 | tf_op jit(solution)/shard_map/all_gather | solution.py:176
  228.2 2.3 fusion.66
  231.1 10.8 %while.29 = (s32[]{:T(128)}, f32[4,64,64]{2,1,0:T(8,128)S(1)}, f32[2,64,4,64]{1,0,3,2:T(2,128)}, f32[2,64,4,64]{1,0,3,2:T(2,128)S(1)}, f32[2,64,4,64]{3,2,1,0:T(...) while((s32[]{:T(128)}, f32[4,64,64]{2,1,0:T(8,128)S(1)}, ...), condition=%wide.region_3.4_spmd.clone, body=%wide.region_0.3_spmd.clone.sunk | while | flops 51646208 | bytes 3493048 | solution.py:115
  233.1 2.8 dynamic_update_slice.6
  238.4 2.8 dynamic_update_slice.6
  245.2 29.8 %all_gather.35 = f32[32,4,64]{2,1,0:T(4,128)S(1)} all-gather(f32[1,4,64]{2,1,0:T(4,128)S(1)} %all_gather.34), channel_id=1, replica_groups=mesh['seq'=32,'mp'=16] {'seq'}, dimensions={0}, use_global_device_ids=true | all-gather | bytes 33792 | tf_op jit(solution)/shard_map/all_gather | solution.py:41
  276.0 1.1 exponential_multiply_fusion
  280.4 33.3 %all-gather.18.cloned.1.call-done = f32[128,64,64]{2,1,0:T(8,128)} async-done(((f32[4,64,64]{2,1,0:T(8,128)}), f32[128,64,64]{2,1,0:T(8,128)}) %all-gather.18.cloned.1.call-update) | async-done | bytes 2097168 | tf_op jit(solution)/shard_map/all_gather | solution.py:41
  313.7 33.7 %while.30 = (s32[]{:T(128)}, f32[4,64]{1,0:T(4,128)S(1)}, f32[4,64,64]{2,1,0:T(8,128)S(1)}, s32[]{:T(128)}, f32[32,4,64]{2,1,0:T(4,128)S(1)}, /*index=5*/f32[32,4,64,64]{3,2,1,0:T(8,128)}, s32[]{:T(128)}, s32[]{:T(128)}) while((s32[]{:T(128)}, f32[4,64]{1,0:T(4,128)S(1)}, f32[4,64,64]{2,1,0:T(8,128)S(1)}, s32[]{:T(128)}, ...), condition=%wide.region_6.7_spmd.clone, body=%wide.region_5.6_spmd.clone.sunk | while | flops 66308 | bytes 201843 | solution.py:50
  327.8 1.1 fusion.106
  347.4 1.8 fusion.27
  349.7 34.3 %all-gather.14.cloned.1.call-done = bf16[4096,256]{1,0:T(8,128)(2,1)} async-done(((bf16[128,256]{1,0:T(8,128)(2,1)}), bf16[4096,256]{1,0:T(8,128)(2,1)}) %all-gather.14.cloned.1.call-update) | async-done | bytes 2097168 | tf_op jit(solution)/shard_map/all_gather | solution.py:177
  384.1 72.4 %all-gather.16.cloned.1.call-done = bf16[256,4096]{1,0:T(8,128)(2,1)} async-done(((bf16[256,128]{1,0:T(8,128)(2,1)}), bf16[256,4096]{1,0:T(8,128)(2,1)}) %all-gather.16.cloned.1.call-update) | async-done | bytes 2097168 | tf_op jit(solution)/shard_map/all_gather | solution.py:256
  456.5 6.6 %fusion.43 = f32[256,4096]{1,0:T(8,128)} fusion(bf16[256,4096]{1,0:T(8,128)(2,1)} %all-gather.16.cloned.1.call-done, f32[256,256]{1,0:T(8,128)S(1)} %copy.147, f32[256,256]{1,0:T(8,128)S(1)} %copy.146, f32[128,256]{1,0:T(8,128)S(1)} %concatenate.27, f32[128,256]{1,0:T(8,128)S(1)} %copy.144, f32[256]{0:T(256)S(1)} %copy-done.21, f32[256]{0:T(256)S(1)} %copy-done.22, ...), kind=kOutput, calls=%fused_computation.84 | convolution fusion | flops 1074528256 | bytes 11274496 | tf_op jit(solution)/shard_map/dot_general | solution.py:258
  464.6 1.3 convolution_add_fusion.1
  466.7 85.1 %reduce-scatter.2.cloned.1.call-done = f32[16,4096]{1,0:T(8,128)} async-done(((f32[256,4096]{1,0:T(8,128)}), f32[16,4096]{1,0:T(8,128)}) %reduce-scatter.2.cloned.1.call-update) | async-done | bytes 262160 | tf_op jit(solution)/shard_map/reduce_scatter | solution.py:257
  551.8 1.6 convert_bitcast_fusion
  (252 shorter events, 69.2 us)
Async XLA Ops:
  7.2 146.6 %copy-start = (bf16[4096,128]{1,0:T(8,128)(2,1)S(1)}, bf16[4096,128]{1,0:T(8,128)(2,1)}, u32[]{:S(2)}) copy-start(bf16[4096,128]{1,0:T(8,128)(2,1)} %param.32) | copy-start | bytes 3145732
  7.2 160.3 %all-gather.12.cloned.1.call-start = ((), (), s32[]{:S(2)}) async-start(), calls=%async_computation.3 | async-start | bytes 2162688 | tf_op jit(solution)/shard_map/all_gather | solution.py:174
  7.9 163.4 %all-gather.8.cloned.1.call-start = ((), (), s32[]{:S(2)}) async-start(), calls=%async_computation.1 | async-start | bytes 2162688 | tf_op jit(solution)/shard_map/all_gather | solution.py:175
  8.7 219.5 %all-gather.10.cloned.1.call-start = ((), (), s32[]{:S(2)}) async-start(), calls=%async_computation.2 | async-start | bytes 2162688 | tf_op jit(solution)/shard_map/all_gather | solution.py:176
  10.4 10.7 %collective-permute-start = (bf16[256,256]{1,0:T(8,128)(2,1)S(1)}, bf16[256,256]{1,0:T(8,128)(2,1)S(1)}, u32[]{:S(2)}, u32[]{:S(2)}) collective-permute-start(bf16[256,256]{1,0:T(8,128)(2,1)S(1)} %constant_dynamic-update-slice_fusion), channel_id=1, source_target_pairs={{0,1},{1,2},{2,3},{3,4},{4,5},{5,6},{6,7},{7,8},{8,9},{9,10},{10,1... | collective-permute-start | bytes 393224 | tf_op jit(solution)/shard_map/ppermute | solution.py:24
  21.1 10.2 %collective-permute-start.1 = (bf16[256,256]{1,0:T(8,128)(2,1)S(1)}, bf16[256,256]{1,0:T(8,128)(2,1)S(1)}, u32[]{:S(2)}, u32[]{:S(2)}) collective-permute-start(bf16[256,256]{1,0:T(8,128)(2,1)S(1)} %collective-permute-done), channel_id=1, source_target_pairs={{0,1},{1,2},{2,3},{3,4},{4,5},{5,6},{6,7},{7,8},{8,9},{9,10},{10,1... | collective-permute-start | bytes 393224 | tf_op jit(solution)/shard_map/ppermute | solution.py:24
  23.1 10.2 %collective-permute-start.8 = (bf16[256,256]{1,0:T(8,128)(2,1)S(1)}, bf16[256,256]{1,0:T(8,128)(2,1)S(1)}, u32[]{:S(2)}, u32[]{:S(2)}) collective-permute-start(bf16[256,256]{1,0:T(8,128)(2,1)S(1)} %constant_dynamic-update-slice_fusion), channel_id=1, source_target_pairs={{1,0},{2,1},{3,2},{4,3},{5,4},{6,5},{7,6},{8,7},{9,8},{10,9},{11,1... | collective-permute-start | bytes 393224 | tf_op jit(solution)/shard_map/ppermute | solution.py:26
  31.3 11.0 %collective-permute-start.2 = (bf16[256,256]{1,0:T(8,128)(2,1)S(1)}, bf16[256,256]{1,0:T(8,128)(2,1)S(1)}, u32[]{:S(2)}, u32[]{:S(2)}) collective-permute-start(bf16[256,256]{1,0:T(8,128)(2,1)S(1)} %collective-permute-done.1), channel_id=1, source_target_pairs={{0,1},{1,2},{2,3},{3,4},{4,5},{5,6},{6,7},{7,8},{8,9},{9,10},{10,1... | collective-permute-start | bytes 393224 | tf_op jit(solution)/shard_map/ppermute | solution.py:24
  33.2 11.0 %collective-permute-start.9 = (bf16[256,256]{1,0:T(8,128)(2,1)S(1)}, bf16[256,256]{1,0:T(8,128)(2,1)S(1)}, u32[]{:S(2)}, u32[]{:S(2)}) collective-permute-start(bf16[256,256]{1,0:T(8,128)(2,1)S(1)} %collective-permute-done.8), channel_id=1, source_target_pairs={{1,0},{2,1},{3,2},{4,3},{5,4},{6,5},{7,6},{8,7},{9,8},{10,9},{11,1... | collective-permute-start | bytes 393224 | tf_op jit(solution)/shard_map/ppermute | solution.py:26
  42.3 11.3 %collective-permute-start.3 = (bf16[256,256]{1,0:T(8,128)(2,1)S(1)}, bf16[256,256]{1,0:T(8,128)(2,1)S(1)}, u32[]{:S(2)}, u32[]{:S(2)}) collective-permute-start(bf16[256,256]{1,0:T(8,128)(2,1)S(1)} %collective-permute-done.2), channel_id=1, source_target_pairs={{0,1},{1,2},{2,3},{3,4},{4,5},{5,6},{6,7},{7,8},{8,9},{9,10},{10,1... | collective-permute-start | bytes 393224 | tf_op jit(solution)/shard_map/ppermute | solution.py:24
  44.2 13.5 %collective-permute-start.10 = (bf16[256,256]{1,0:T(8,128)(2,1)S(1)}, bf16[256,256]{1,0:T(8,128)(2,1)S(1)}, u32[]{:S(2)}, u32[]{:S(2)}) collective-permute-start(bf16[256,256]{1,0:T(8,128)(2,1)S(1)} %collective-permute-done.9), channel_id=1, source_target_pairs={{1,0},{2,1},{3,2},{4,3},{5,4},{6,5},{7,6},{8,7},{9,8},{10,9},{11,1... | collective-permute-start | bytes 393224 | tf_op jit(solution)/shard_map/ppermute | solution.py:26
  53.6 11.1 %collective-permute-start.4 = (bf16[256,256]{1,0:T(8,128)(2,1)S(1)}, bf16[256,256]{1,0:T(8,128)(2,1)S(1)}, u32[]{:S(2)}, u32[]{:S(2)}) collective-permute-start(bf16[256,256]{1,0:T(8,128)(2,1)S(1)} %collective-permute-done.3), channel_id=1, source_target_pairs={{0,1},{1,2},{2,3},{3,4},{4,5},{5,6},{6,7},{7,8},{8,9},{9,10},{10,1... | collective-permute-start | bytes 393224 | tf_op jit(solution)/shard_map/ppermute | solution.py:24
  56.4 31.7 %collective-permute-start.15 = (bf16[1,256]{0,1:T(8,128)(2,1)S(1)}, bf16[1,256]{0,1:T(8,128)(2,1)S(1)}, u32[]{:S(2)}, u32[]{:S(2)}) collective-permute-start(bf16[1,256]{0,1:T(8,128)(2,1)S(1)} %copy.120), channel_id=1, source_target_pairs={{0,16},{16,32},{32,48},{48,64},{64,80},{80,96},{96,112},{112,128},... | collective-permute-start | bytes 1544 | tf_op jit(solution)/shard_map/ppermute | solution.py:36
  57.7 256.0 %all-gather.18.cloned.1.call-start = ((), (), s32[]{:S(2)}) async-start(), calls=%async_computation.7 | async-start | bytes 4325376 | tf_op jit(solution)/shard_map/all_gather | solution.py:41
  57.8 11.0 %collective-permute-start.11 = (bf16[256,256]{1,0:T(8,128)(2,1)S(1)}, bf16[256,256]{1,0:T(8,128)(2,1)S(1)}, u32[]{:S(2)}, u32[]{:S(2)}) collective-permute-start(bf16[256,256]{1,0:T(8,128)(2,1)S(1)} %collective-permute-done.10), channel_id=1, source_target_pairs={{1,0},{2,1},{3,2},{4,3},{5,4},{6,5},{7,6},{8,7},{9,8},{10,9},{11,1... | collective-permute-start | bytes 393224 | tf_op jit(solution)/shard_map/ppermute | solution.py:26
  64.7 11.2 %collective-permute-start.5 = (bf16[256,256]{1,0:T(8,128)(2,1)S(1)}, bf16[256,256]{1,0:T(8,128)(2,1)S(1)}, u32[]{:S(2)}, u32[]{:S(2)}) collective-permute-start(bf16[256,256]{1,0:T(8,128)(2,1)S(1)} %collective-permute-done.4), channel_id=1, source_target_pairs={{0,1},{1,2},{2,3},{3,4},{4,5},{5,6},{6,7},{7,8},{8,9},{9,10},{10,1... | collective-permute-start | bytes 393224 | tf_op jit(solution)/shard_map/ppermute | solution.py:24
  68.7 9.7 %collective-permute-start.12 = (bf16[256,256]{1,0:T(8,128)(2,1)S(1)}, bf16[256,256]{1,0:T(8,128)(2,1)S(1)}, u32[]{:S(2)}, u32[]{:S(2)}) collective-permute-start(bf16[256,256]{1,0:T(8,128)(2,1)S(1)} %collective-permute-done.11), channel_id=1, source_target_pairs={{1,0},{2,1},{3,2},{4,3},{5,4},{6,5},{7,6},{8,7},{9,8},{10,9},{11,1... | collective-permute-start | bytes 393224 | tf_op jit(solution)/shard_map/ppermute | solution.py:26
  76.0 10.2 %collective-permute-start.6 = (bf16[256,256]{1,0:T(8,128)(2,1)S(1)}, bf16[256,256]{1,0:T(8,128)(2,1)S(1)}, u32[]{:S(2)}, u32[]{:S(2)}) collective-permute-start(bf16[256,256]{1,0:T(8,128)(2,1)S(1)} %collective-permute-done.5), channel_id=1, source_target_pairs={{0,1},{1,2},{2,3},{3,4},{4,5},{5,6},{6,7},{7,8},{8,9},{9,10},{10,1... | collective-permute-start | bytes 393224 | tf_op jit(solution)/shard_map/ppermute | solution.py:24
  78.5 42.0 %collective-permute-start.13 = (bf16[256,256]{1,0:T(8,128)(2,1)S(1)}, bf16[256,256]{1,0:T(8,128)(2,1)S(1)}, u32[]{:S(2)}, u32[]{:S(2)}) collective-permute-start(bf16[256,256]{1,0:T(8,128)(2,1)S(1)} %collective-permute-done.12), channel_id=1, source_target_pairs={{1,0},{2,1},{3,2},{4,3},{5,4},{6,5},{7,6},{8,7},{9,8},{10,9},{11,1... | collective-permute-start | bytes 393224 | tf_op jit(solution)/shard_map/ppermute | solution.py:26
  86.2 37.0 %collective-permute-start.7 = (bf16[256,256]{1,0:T(8,128)(2,1)S(1)}, bf16[256,256]{1,0:T(8,128)(2,1)S(1)}, u32[]{:S(2)}, u32[]{:S(2)}) collective-permute-start(bf16[256,256]{1,0:T(8,128)(2,1)S(1)} %collective-permute-done.6), channel_id=1, source_target_pairs={{0,1},{1,2},{2,3},{3,4},{4,5},{5,6},{6,7},{7,8},{8,9},{9,10},{10,1... | collective-permute-start | bytes 393224 | tf_op jit(solution)/shard_map/ppermute | solution.py:24
  120.5 12.5 %collective-permute-start.14 = (bf16[256,256]{1,0:T(8,128)(2,1)S(1)}, bf16[256,256]{1,0:T(8,128)(2,1)S(1)}, u32[]{:S(2)}, u32[]{:S(2)}) collective-permute-start(bf16[256,256]{1,0:T(8,128)(2,1)S(1)} %collective-permute-done.13), channel_id=1, source_target_pairs={{1,0},{2,1},{3,2},{4,3},{5,4},{6,5},{7,6},{8,7},{9,8},{10,9},{11,1... | collective-permute-start | bytes 393224 | tf_op jit(solution)/shard_map/ppermute | solution.py:26
  144.0 5.5 copy-start.4
  157.1 10.3 %copy-start.7 = (f32[128,256]{0,1:T(8,128)}, f32[128,256]{0,1:T(8,128)S(1)}, u32[]{:S(2)}) copy-start(f32[128,256]{0,1:T(8,128)S(1)} %get-tuple-element.286) | copy-start | bytes 393220
  157.1 88.0 %copy-start.19 = (f32[256]{0:T(256)}, f32[256]{0:T(256)S(1)}, u32[]{:S(2)}) copy-start(f32[256]{0:T(256)S(1)} %get-tuple-element.284) | copy-start | bytes 3076
  171.3 56.9 %copy-start.6 = (bf16[256,4096]{0,1:T(8,128)(2,1)S(1)}, bf16[256,4096]{0,1:T(8,128)(2,1)}, u32[]{:S(2)}) copy-start(bf16[256,4096]{0,1:T(8,128)(2,1)} %get-tuple-element.278) | copy-start | bytes 6291460
  228.2 2.9 copy-start.18
  231.1 12.7 %copy-start.23 = (s32[2]{0:T(128)S(1)}, s32[2]{0:T(128)}, u32[]{:S(2)}) copy-start(s32[2]{0:T(128)} %param.23) | copy-start | bytes 28
  231.1 13.4 %copy-start.11 = (f32[128,256]{0,1:T(8,128)S(1)}, f32[128,256]{0,1:T(8,128)}, u32[]{:S(2)}) copy-start(f32[128,256]{0,1:T(8,128)} %get-tuple-element.285) | copy-start | bytes 393220
  231.1 43.9 %copy-start.8 = (f32[128,256]{0,1:T(8,128)S(1)}, f32[128,256]{0,1:T(8,128)}, u32[]{:S(2)}) copy-start(f32[128,256]{0,1:T(8,128)} %copy-done.7) | copy-start | bytes 393220
  231.1 1.9 copy-start.15
  235.8 0.7 copy-start.16
  236.5 1.9 copy-start.15
  241.2 0.7 copy-start.16
  241.9 33.2 %copy-start.12 = (f32[128,256]{0,1:T(8,128)S(1)}, f32[128,256]{0,1:T(8,128)}, u32[]{:S(2)}) copy-start(f32[128,256]{0,1:T(8,128)} %get-tuple-element.288) | copy-start | bytes 393220
  241.9 33.6 %copy-start.13 = (f32[128,256]{1,0:T(8,128)S(1)}, f32[128,256]{1,0:T(8,128)}, u32[]{:S(2)}) copy-start(f32[128,256]{1,0:T(8,128)} %get-tuple-element.292) | copy-start | bytes 393220
  242.6 141.5 %all-gather.14.cloned.1.call-start = ((), (), s32[]{:S(2)}) async-start(), calls=%async_computation.4 | async-start | bytes 2162688 | tf_op jit(solution)/shard_map/all_gather | solution.py:177
  243.2 213.3 %all-gather.16.cloned.1.call-start = ((), (), s32[]{:S(2)}) async-start(), calls=%async_computation.5 | async-start | bytes 2162688 | tf_op jit(solution)/shard_map/all_gather | solution.py:256
  243.7 308.0 %reduce-scatter.2.cloned.1.call-start = ((), (), s32[]{:S(2)}) async-start(), calls=%async_computation.6 | async-start | bytes 4456448 | tf_op jit(solution)/shard_map/reduce_scatter | solution.py:257
  245.1 32.0 %copy-start.9 = (f32[2,64,4,64]{3,2,1,0:T(4,128)}, f32[2,64,4,64]{3,2,1,0:T(4,128)S(1)}, u32[]{:S(2)}) copy-start(f32[2,64,4,64]{3,2,1,0:T(4,128)S(1)} %fusion.40) | copy-start | bytes 393220
  277.1 2.6 copy-start.17
  347.4 109.1 %copy-start.5 = (bf16[256,4096]{0,1:T(8,128)(2,1)S(1)}, bf16[256,4096]{0,1:T(8,128)(2,1)}, u32[]{:S(2)}) copy-start(bf16[256,4096]{0,1:T(8,128)(2,1)} %get-tuple-element.276) | copy-start | bytes 6291460
  347.4 109.1 %copy-start.21 = (f32[256]{0:T(256)S(1)}, f32[256]{0:T(256)}, u32[]{:S(2)}) copy-start(f32[256]{0:T(256)} %param.36) | copy-start | bytes 3076
  347.4 109.1 %copy-start.22 = (f32[256]{0:T(256)S(1)}, f32[256]{0:T(256)}, u32[]{:S(2)}) copy-start(f32[256]{0:T(256)} %param.35) | copy-start | bytes 3076
  463.1 90.3 %copy-start.1 = (bf16[4096,128]{1,0:T(8,128)(2,1)S(1)}, bf16[4096,128]{1,0:T(8,128)(2,1)}, u32[]{:S(2)}) copy-start(bf16[4096,128]{1,0:T(8,128)(2,1)} %param.32) | copy-start | bytes 3145732
  463.1 0.8 copy-start.20
  463.1 1.5 copy-start.10
  463.1 2.9 copy-start.3
  463.1 2.9 copy-start.14
  (1 other events, 0.6 us)
Sparse Core Ops, SparseCore 0:
  10.1 76.2 all-gather.11
  88.6 68.5 all-gather.7
  159.3 68.8 all-gather.9
  242.7 70.9 all-gather.17
  315.6 68.3 all-gather.13
  386.0 70.4 all-gather.15
  463.2 88.5 reduce-scatter.1
